TPU v7x, 32 devices: a whole 2x2x4 slice. The times are simulated.
32 devices in a mesh: parts: 2 (over x), tm: 16 (over z, y, core).
Axes of the slice: x: 2, y: 2, z: 4, core: 2. Of those that a mesh axis runs over, the one named last changes fastest.
Arguments:
- query_states: bfloat16 [32, 384, 768], P(('parts', 'tm')), parts along dimension 0, may hold values from -88 to 88
- key_states: bfloat16 [32, 384, 768], P(('parts', 'tm')), parts along dimension 0, may hold values from -4 to 4
- value_states: bfloat16 [32, 384, 768], P(('parts', 'tm')), parts along dimension 0, may hold values from -40 to 40
- out_weight: bfloat16 [1536, 3072], replicated, may hold values from -0.15625 to 0.15625
Outputs:
- mixed: bfloat16 [6144, 3072], P(('parts', 'tm')), parts along dimension 0
There are 2 independent parts, one for each index of `parts`. A program takes and returns all parts, laid end to end along the dimension named above; an argument that names none is the same for every part. Nothing has to cross between parts.
All inputs are finite; a program needn't handle non-finite values.
Results may differ from a plain program's by a relative error of at most 0.0058.
Values may be sent and summed in bfloat16 or wider, within the bound.
A program may use at most 128 MiB of HBM per device.

v0:
```python
import jax
import jax.numpy as jnp
from jax import lax
from jax.sharding import PartitionSpec as P

TCOLS = 4
HD = 128


masked_score = -1e30


def from_behind(block, axis, distance):
    devices = range(lax.axis_size(axis))
    route = [(i - distance, i) for i in devices if i - distance in devices]
    return lax.ppermute(block, axis, route)


def swapped(shard, axis, bit):
    return lax.ppermute(shard, axis, [(i, i ^ 1 << bit) for i in range(lax.axis_size(axis))])


def tile_from(stacked, offset):
    return from_behind(stacked, "tm", -2 * offset)


def window_direct(stacked):
    blocks = []
    for time_step in (-1, 0, 1):
        for col_step in (-1, 0, 1):
            if time_step == 0 and col_step == 0:
                blocks.append(stacked)
            else:
                blocks.append(tile_from(stacked, time_step * TCOLS + col_step))
    return jnp.concatenate(blocks, axis=1)


def window_attention(query_tile, key_window, value_window, key_ok):
    score_scale = HD ** (-0.5)
    tile_rows = query_tile.shape[0]
    key_rows = key_window.shape[0]
    heads_here = query_tile.shape[1] // HD
    per_step = 2
    pieces = []
    for head_start in range(0, heads_here, per_step):
        first_col = head_start * HD
        last_col = first_col + per_step * HD
        query_part = query_tile[:, first_col:last_col].reshape(tile_rows, per_step, HD)
        key_part = key_window[:, first_col:last_col].reshape(key_rows, per_step, HD)
        value_part = value_window[:, first_col:last_col].reshape(key_rows, per_step, HD)
        scores = (
            lax.dot_general(
                query_part,
                key_part,
                (((2,), (2,)), ((1,), (1,))),
                preferred_element_type=jnp.float32,
            )
            * score_scale
        )
        scores = jnp.where(key_ok[None, None, :], scores, masked_score)
        row_max = jnp.max(scores, axis=2, keepdims=True)
        exp_scores = jnp.exp(scores - row_max)
        denominator = jnp.sum(exp_scores, axis=2, keepdims=True)
        weights = (exp_scores / denominator).astype(jnp.bfloat16)
        result = lax.dot_general(
            weights, value_part, (((2,), (0,)), ((0,), (1,))), preferred_element_type=jnp.float32
        )
        result = result.astype(jnp.bfloat16).transpose(1, 0, 2).reshape(tile_rows, per_step * HD)
        pieces.append(result)
    return jnp.concatenate(pieces, axis=1)


def per_device(query_states, key_states, value_states, out_weight):
    query_tile = query_states[0]
    key_tile = key_states[0]
    value_tile = value_states[0]
    tile_rows = query_tile.shape[0]
    half_width = query_tile.shape[1]
    half_rows = tile_rows // 2
    position = lax.axis_index("tm")
    device_count = lax.axis_size("tm")
    head_group = position % 2
    other_group = 1 - head_group
    tile_index = position // 2
    col_tile = tile_index % TCOLS
    time_tile = tile_index // TCOLS
    time_count = device_count // (2 * TCOLS)
    stacked = jnp.stack((key_tile, value_tile))
    window_stack = window_direct(stacked)
    tile_steps = jnp.arange(3, dtype=jnp.int32) - 1
    time_ok = (time_tile + tile_steps >= 0) & (time_tile + tile_steps < time_count)
    col_ok = (col_tile + tile_steps >= 0) & (col_tile + tile_steps < TCOLS)
    tile_ok = (time_ok[:, None] & col_ok[None, :]).reshape(9)
    key_ok = jnp.repeat(tile_ok, tile_rows)
    attended = window_attention(query_tile, window_stack[0], window_stack[1], key_ok)
    weight_own = lax.dynamic_slice_in_dim(out_weight, head_group * half_width, half_width, 0)
    own_attended = lax.dynamic_slice_in_dim(attended, head_group * half_rows, half_rows, 0)
    other_attended = lax.dynamic_slice_in_dim(attended, other_group * half_rows, half_rows, 0)
    received = swapped(other_attended, "tm", 0)
    weight_other = lax.dynamic_slice_in_dim(out_weight, other_group * half_width, half_width, 0)
    mixed_rows = jnp.dot(own_attended, weight_own, preferred_element_type=jnp.float32) + jnp.dot(
        received, weight_other, preferred_element_type=jnp.float32
    )
    return mixed_rows.astype(jnp.bfloat16)


def solution(mesh):
    in_specs = (
        P(("parts", "tm"), None, None),
        P(("parts", "tm"), None, None),
        P(("parts", "tm"), None, None),
        P(),
    )
    out_specs = P(("parts", "tm"), None)
    return jax.shard_map(
        per_device, mesh=mesh, in_specs=in_specs, out_specs=out_specs, check_vma=False
    )
```

profile of v0, /device:TPU:0, one launch (start us, length us, event | category | flops | bytes accessed | tf_op | source)
XLA Modules:
  0.0 298.3 jit_solution(15766207930555600884)
XLA Ops:
  2.9 8.0 %collective-permute-start = (bf16[2,384,768]{1,2,0:T(8,128)(2,1)S(1)}, bf16[2,384,768]{1,2,0:T(8,128)(2,1)}, u32[]{:S(2)}, u32[]{:S(2)}) collective-permute-start(bf16[2,384,768]{1,2,0:T(8,128)(2,1)S(1)} %pad_maximum_fusion), channel_id=1, source_target_pairs={{0,10},{1,11},{2,12},{3,13},{4,14},{5,15},{16,26},{17,27},{18,28},... | collective-permute-start | bytes 3538952 | tf_op jit(solution)/shard_map/ppermute | solution.py:16
  13.2 3.5 %collective-permute-start.2 = (bf16[2,384,768]{1,2,0:T(8,128)(2,1)S(1)}, bf16[2,384,768]{1,2,0:T(8,128)(2,1)}, u32[]{:S(2)}, u32[]{:S(2)}) collective-permute-start(bf16[2,384,768]{1,2,0:T(8,128)(2,1)S(1)} %pad_maximum_fusion), channel_id=1, source_target_pairs={{0,6},{1,7},{2,8},{3,9},{4,10},{5,11},{6,12},{7,13},{8,14},{9,15},... | collective-permute-start | bytes 3538952 | tf_op jit(solution)/shard_map/ppermute | solution.py:16
  16.7 3.3 %collective-permute-start.3 = (bf16[2,384,768]{1,2,0:T(8,128)(2,1)S(1)}, bf16[2,384,768]{1,2,0:T(8,128)(2,1)}, u32[]{:S(2)}, u32[]{:S(2)}) collective-permute-start(bf16[2,384,768]{1,2,0:T(8,128)(2,1)S(1)} %pad_maximum_fusion), channel_id=1, source_target_pairs={{0,2},{1,3},{2,4},{3,5},{4,6},{5,7},{6,8},{7,9},{8,10},{9,11},{10,... | collective-permute-start | bytes 3538952 | tf_op jit(solution)/shard_map/ppermute | solution.py:16
  23.5 26.7 %collective-permute-done = bf16[2,384,768]{1,2,0:T(8,128)(2,1)} collective-permute-done((bf16[2,384,768]{1,2,0:T(8,128)(2,1)S(1)}, bf16[2,384,768]{1,2,0:T(8,128)(2,1)}, u32[]{:S(2)}, u32[]{:S(2)}) %collective-permute-start) | collective-permute-done | bytes 1179680 | tf_op jit(solution)/shard_map/ppermute | solution.py:16
  51.5 24.0 %collective-permute-done.1 = bf16[2,384,768]{1,2,0:T(8,128)(2,1)} collective-permute-done((bf16[2,384,768]{1,2,0:T(8,128)(2,1)S(1)}, bf16[2,384,768]{1,2,0:T(8,128)(2,1)}, u32[]{:S(2)}, u32[]{:S(2)}) %collective-permute-start.1) | collective-permute-done | bytes 1179680 | tf_op jit(solution)/shard_map/ppermute | solution.py:16
  76.8 35.2 %collective-permute-done.2 = bf16[2,384,768]{1,2,0:T(8,128)(2,1)} collective-permute-done((bf16[2,384,768]{1,2,0:T(8,128)(2,1)S(1)}, bf16[2,384,768]{1,2,0:T(8,128)(2,1)}, u32[]{:S(2)}, u32[]{:S(2)}) %collective-permute-start.2) | collective-permute-done | bytes 1179680 | tf_op jit(solution)/shard_map/ppermute | solution.py:16
  113.5 2.5 constant_dynamic-update-slice_fusion.8
  116.0 2.4 constant_dynamic-update-slice_fusion.7
  118.4 2.5 constant_dynamic-update-slice_fusion.6
  120.9 2.5 constant_dynamic-update-slice_fusion.5
  124.5 2.4 constant_dynamic-update-slice_fusion.3
  127.0 2.5 constant_dynamic-update-slice_fusion.2
  129.5 43.5 %collective-permute-done.6 = bf16[2,384,768]{1,2,0:T(8,128)(2,1)} collective-permute-done((bf16[2,384,768]{1,2,0:T(8,128)(2,1)S(1)}, bf16[2,384,768]{1,2,0:T(8,128)(2,1)}, u32[]{:S(2)}, u32[]{:S(2)}) %collective-permute-start.6) | collective-permute-done | bytes 1179680 | tf_op jit(solution)/shard_map/ppermute | solution.py:16
  173.0 2.5 constant_dynamic-update-slice_fusion.1
  175.4 55.7 %collective-permute-done.7 = bf16[2,384,768]{1,2,0:T(8,128)(2,1)} collective-permute-done((bf16[2,384,768]{1,2,0:T(8,128)(2,1)S(1)}, bf16[2,384,768]{1,2,0:T(8,128)(2,1)}, u32[]{:S(2)}, u32[]{:S(2)}) %collective-permute-start.7) | collective-permute-done | bytes 1179680 | tf_op jit(solution)/shard_map/ppermute | solution.py:16
  231.2 2.5 constant_dynamic-update-slice_fusion
  233.6 8.7 %slice_bitcast_fusion = (bf16[3456,768]{0,1:T(8,128)(2,1)}, bf16[3456,768]{0,1:T(8,128)(2,1)}) fusion(bf16[2,3456,768]{1,2,0:T(8,128)(2,1)} %constant_dynamic-update-slice_fusion), kind=kLoop, calls=%fused_computation.21 | loop fusion | bytes 21233664 | tf_op jit(solution)/shard_map/squeeze | solution.py:95
  242.3 7.3 %fusion.55 = (bf16[3456,256]{0,1:T(8,128)(2,1)}, bf16[3456,256]{0,1:T(8,128)(2,1)}, bf16[3456,256]{0,1:T(8,128)(2,1)}, bf16[3456,256]{0,1:T(8,128)(2,1)S(1)}, bf...) fusion(bf16[3456,768]{0,1:T(8,128)(2,1)} %get-tuple-element.5, bf16[3456,768]{0,1:T(8,128)(2,1)} %get-tuple-element.6), kind=kLoop, calls=%fused_computation.72 | loop fusion | bytes 21233664 | tf_op jit(solution)/shard_map/slice | solution.py:49
  249.6 9.4 %fusion.60 = (f32[2,384]{1,0:T(2,128)S(1)}, f32[2,384,3456]{1,2,0:T(8,128)}) fusion(pred[3456]{0:T(1024)(128)(4,1)S(1)} %broadcast_in_dim.34, bf16[3456,2,128]{0,2,1:T(8,128)(2,1)} %bitcast.78, bf16[384,2,128]{0,2,1:T(8,128)(2,1)} %bitcast.81), kind=kOutput, calls=%fused_computation.77 | convolution fusion | flops 690097536 | bytes 12589440 | tf_op jit(solution)/shard_map/sub | solution.py:62
  259.0 9.2 %fusion.59 = (f32[2,384]{1,0:T(2,128)S(1)}, f32[2,384,3456]{1,2,0:T(8,128)}) fusion(pred[3456]{0:T(1024)(128)(4,1)S(1)} %broadcast_in_dim.34, bf16[3456,2,128]{0,2,1:T(8,128)(2,1)} %bitcast.77, bf16[384,2,128]{0,2,1:T(8,128)(2,1)} %bitcast.80), kind=kOutput, calls=%fused_computation.76 | convolution fusion | flops 690097536 | bytes 12589440 | tf_op jit(solution)/shard_map/sub | solution.py:62
  268.2 9.6 %fusion.58 = (f32[2,384]{1,0:T(2,128)S(1)}, f32[2,384,3456]{1,2,0:T(8,128)}) fusion(pred[3456]{0:T(1024)(128)(4,1)S(1)} %broadcast_in_dim.34, bf16[3456,2,128]{0,2,1:T(8,128)(2,1)} %bitcast.76, bf16[384,2,128]{0,2,1:T(8,128)(2,1)} %bitcast.79), kind=kOutput, calls=%fused_computation.75 | convolution fusion | flops 690097536 | bytes 12589440 | tf_op jit(solution)/shard_map/sub | solution.py:62
  277.8 5.8 %fusion.39 = bf16[2,384,128]{1,2,0:T(8,128)(2,1)S(1)} fusion(bf16[3456,2,128]{0,2,1:T(8,128)(2,1)} %bitcast.75, f32[2,384,3456]{1,2,0:T(8,128)} %get-tuple-element.21, f32[2,384]{1,0:T(2,128)S(1)} %get-tuple-element.20), kind=kOutput, calls=%fused_computation.44 | convolution fusion | flops 684883968 | bytes 12585984 | tf_op jit(solution)/shard_map/dot_general | solution.py:65
  290.2 3.6 %fusion.29 = f32[192,3072]{1,0:T(8,128)S(1)} fusion(bf16[1536,3072]{1,0:T(8,128)(2,1)} %param.7, s32[]{:T(128)S(6)} %select_n.60, bf16[384,768]{0,1:T(8,128)(2,1)S(1)} %pad_maximum_fusion.1, s32[]{:T(128)S(6)} %select_n.59), kind=kOutput, calls=%fused_computation.37 | convolution fusion | flops 905969664 | bytes 7471112 | tf_op jit(solution)/shard_map/dot_general | solution.py:101
  293.8 4.5 %fusion.34 = bf16[192,3072]{1,0:T(8,128)(2,1)} fusion(f32[192,3072]{1,0:T(8,128)S(1)} %fusion.29, bf16[192,768]{0,1:T(8,128)(2,1)S(1)} %collective-permute-done.8, bf16[1536,3072]{1,0:T(8,128)(2,1)} %param.7, s32[]{:T(128)S(6)} %select_n.62), kind=kOutput, calls=%fused_computation.40 | convolution fusion | flops 907149312 | bytes 8552452 | tf_op jit(solution)/shard_map/dot_general | solution.py:101
  (34 shorter events, 20.5 us)
Async XLA Ops:
  2.9 47.3 %collective-permute-start = (bf16[2,384,768]{1,2,0:T(8,128)(2,1)S(1)}, bf16[2,384,768]{1,2,0:T(8,128)(2,1)}, u32[]{:S(2)}, u32[]{:S(2)}) collective-permute-start(bf16[2,384,768]{1,2,0:T(8,128)(2,1)S(1)} %pad_maximum_fusion), channel_id=1, source_target_pairs={{0,10},{1,11},{2,12},{3,13},{4,14},{5,15},{16,26},{17,27},{18,28},... | collective-permute-start | bytes 3538952 | tf_op jit(solution)/shard_map/ppermute | solution.py:16
  10.8 64.7 %collective-permute-start.1 = (bf16[2,384,768]{1,2,0:T(8,128)(2,1)S(1)}, bf16[2,384,768]{1,2,0:T(8,128)(2,1)}, u32[]{:S(2)}, u32[]{:S(2)}) collective-permute-start(bf16[2,384,768]{1,2,0:T(8,128)(2,1)S(1)} %pad_maximum_fusion), channel_id=1, source_target_pairs={{0,8},{1,9},{2,10},{3,11},{4,12},{5,13},{6,14},{7,15},{16,24},{17,... | collective-permute-start | bytes 3538952 | tf_op jit(solution)/shard_map/ppermute | solution.py:16
  13.2 98.8 %collective-permute-start.2 = (bf16[2,384,768]{1,2,0:T(8,128)(2,1)S(1)}, bf16[2,384,768]{1,2,0:T(8,128)(2,1)}, u32[]{:S(2)}, u32[]{:S(2)}) collective-permute-start(bf16[2,384,768]{1,2,0:T(8,128)(2,1)S(1)} %pad_maximum_fusion), channel_id=1, source_target_pairs={{0,6},{1,7},{2,8},{3,9},{4,10},{5,11},{6,12},{7,13},{8,14},{9,15},... | collective-permute-start | bytes 3538952 | tf_op jit(solution)/shard_map/ppermute | solution.py:16
  16.7 104.2 %collective-permute-start.3 = (bf16[2,384,768]{1,2,0:T(8,128)(2,1)S(1)}, bf16[2,384,768]{1,2,0:T(8,128)(2,1)}, u32[]{:S(2)}, u32[]{:S(2)}) collective-permute-start(bf16[2,384,768]{1,2,0:T(8,128)(2,1)S(1)} %pad_maximum_fusion), channel_id=1, source_target_pairs={{0,2},{1,3},{2,4},{3,5},{4,6},{5,7},{6,8},{7,9},{8,10},{9,11},{10,... | collective-permute-start | bytes 3538952 | tf_op jit(solution)/shard_map/ppermute | solution.py:16
  20.0 104.6 %collective-permute-start.4 = (bf16[2,384,768]{1,2,0:T(8,128)(2,1)S(1)}, bf16[2,384,768]{1,2,0:T(8,128)(2,1)}, u32[]{:S(2)}, u32[]{:S(2)}) collective-permute-start(bf16[2,384,768]{1,2,0:T(8,128)(2,1)S(1)} %pad_maximum_fusion), channel_id=1, source_target_pairs={{2,0},{3,1},{4,2},{5,3},{6,4},{7,5},{8,6},{9,7},{10,8},{11,9},{12,... | collective-permute-start | bytes 3538952 | tf_op jit(solution)/shard_map/ppermute | solution.py:16
  50.2 76.7 %collective-permute-start.5 = (bf16[2,384,768]{1,2,0:T(8,128)(2,1)S(1)}, bf16[2,384,768]{1,2,0:T(8,128)(2,1)}, u32[]{:S(2)}, u32[]{:S(2)}) collective-permute-start(bf16[2,384,768]{1,2,0:T(8,128)(2,1)S(1)} %pad_maximum_fusion), channel_id=1, source_target_pairs={{6,0},{7,1},{8,2},{9,3},{10,4},{11,5},{12,6},{13,7},{14,8},{15,9},... | collective-permute-start | bytes 3538952 | tf_op jit(solution)/shard_map/ppermute | solution.py:16
  75.5 97.5 %collective-permute-start.6 = (bf16[2,384,768]{1,2,0:T(8,128)(2,1)S(1)}, bf16[2,384,768]{1,2,0:T(8,128)(2,1)}, u32[]{:S(2)}, u32[]{:S(2)}) collective-permute-start(bf16[2,384,768]{1,2,0:T(8,128)(2,1)S(1)} %pad_maximum_fusion), channel_id=1, source_target_pairs={{8,0},{9,1},{10,2},{11,3},{12,4},{13,5},{14,6},{15,7},{24,16},{25,... | collective-permute-start | bytes 3538952 | tf_op jit(solution)/shard_map/ppermute | solution.py:16
  112.0 119.2 %collective-permute-start.7 = (bf16[2,384,768]{1,2,0:T(8,128)(2,1)S(1)}, bf16[2,384,768]{1,2,0:T(8,128)(2,1)}, u32[]{:S(2)}, u32[]{:S(2)}) collective-permute-start(bf16[2,384,768]{1,2,0:T(8,128)(2,1)S(1)} %pad_maximum_fusion), channel_id=1, source_target_pairs={{10,0},{11,1},{12,2},{13,3},{14,4},{15,5},{26,16},{27,17},{28,18},... | collective-permute-start | bytes 3538952 | tf_op jit(solution)/shard_map/ppermute | solution.py:16
  277.8 7.6 %copy-start = (f32[2,384,3456]{1,2,0:T(8,128)S(1)}, f32[2,384,3456]{1,2,0:T(8,128)}, u32[]{:S(2)}) copy-start(f32[2,384,3456]{1,2,0:T(8,128)} %get-tuple-element.19) | copy-start | bytes 31850500
  277.8 8.8 %slice-start = ((s8[10616832]{0:T(1024)(128)(4,1)}), s8[4194304]{0:T(1024)(128)(4,1)S(1)}, s32[]{:S(2)}) async-start(s8[10616832]{0:T(1024)(128)(4,1)} %bitcast.85), calls=%async_computation | async-start | bytes 8388608
  277.8 9.9 %slice-start.1 = ((s8[10616832]{0:T(1024)(128)(4,1)}), s8[4194304]{0:T(1024)(128)(4,1)S(1)}, s32[]{:S(2)}) async-start(s8[10616832]{0:T(1024)(128)(4,1)} %bitcast.85), calls=%async_computation.1 | async-start | bytes 8388608
  285.4 3.3 %slice-start.2 = ((s8[10616832]{0:T(1024)(128)(4,1)}), s8[2228224]{0:T(1024)(128)(4,1)S(1)}, s32[]{:S(2)}) async-start(s8[10616832]{0:T(1024)(128)(4,1)} %bitcast.85), calls=%async_computation.2 | async-start | bytes 4456448
  290.1 3.7 %collective-permute-start.8 = (bf16[192,768]{0,1:T(8,128)(2,1)S(1)}, bf16[192,768]{0,1:T(8,128)(2,1)S(1)}, u32[]{:S(2)}, u32[]{:S(2)}) collective-permute-start(bf16[192,768]{0,1:T(8,128)(2,1)S(1)} %constant_dynamic-slice_fusion), channel_id=1, source_target_pairs={{0,1},{1,0},{2,3},{3,2},{4,5},{5,4},{6,7},{7,6},{8,9},{9,8},{10,11... | collective-permute-start | bytes 884744 | tf_op jit(solution)/shard_map/ppermute | solution.py:20
where the time goes:
time: 299 us; the launch traced here: 298 us
  waiting for transfers between devices  185 us (62%)
  local copies, waits for them, and re-layouts  44.8 us (15%)
  matrix products  44.5 us (15%)
  starting transfers between devices  22.3 us (7%)
    ppermute x8, waiting for transfers between devices, from_behind(): return lax.ppermute(block, axis, route)  185 us
    sub x3, matrix products, window_attention(): exp_scores = jnp.exp(scores - row_max)  28.1 us
    unnamed x18, local copies, waits for them, and re-layouts  25.1 us
    ppermute x8, starting transfers between devices, from_behind(): return lax.ppermute(block, axis, route)  22.2 us
    squeeze x1, local copies, waits for them, and re-layouts, per_device(): window_stack[0]  8.69 us
    dot_general x3, matrix products, window_attention(): lax.dot_general(weights, value_part, (((2,), (0,)), ((0,), (1,))), prefer...  8.23 us
    slice x1, local copies, waits for them, and re-layouts, window_attention(): key_part = key_window[:, first_col:last_col].reshape(key_rows, per_step, HD)  7.32 us
  transfers between devices with their start and end apart: 9, of which 5 were waited for; matrix products, arithmetic and copies ran while one was open for 8% of the time, Pallas kernels for 0%

commit v1 on v0

v1 whole, which is shorter than its diff:
```python
import functools

import jax
import jax.numpy as jnp
from jax import lax
from jax.experimental import pallas as pl
from jax.experimental.pallas import tpu as pltpu
from jax.sharding import PartitionSpec as P

TCOLS = 4
HD = 128
MESH = pl.DeviceIdType.MESH
LOG2E = 1.4426950408889634

DIRECT_OWN = 0
DIRECT_CORNER = 0
LAG = 3


def slot_of(time_step, col_step):
    return (time_step + 1) * 3 + col_step + 1


def kernel(
    time_count,
    heads,
    q_hbm,
    k_hbm,
    v_hbm,
    w_hbm,
    out_ref,
    q_s,
    kv,
    w_s,
    m_s,
    l_s,
    acc_s,
    outgoing,
    attended,
    load_sem,
    w_sem,
    send_sem,
    recv_sem,
    att_send_sem,
    att_recv_sem,
):
    rows = q_s.shape[1]
    half = rows // 2
    me = lax.axis_index("tm")
    group = lax.rem(me, 2)
    tile = lax.div(me, 2)
    col = lax.rem(tile, TCOLS)
    time = lax.div(tile, TCOLS)
    has_time = {-1: time > 0, 1: time < time_count - 1}
    has_col = {-1: col > 0, 1: col < TCOLS - 1}
    outer = 1 - 2 * lax.rem(col, 2)
    is_edge = jnp.logical_or(col == 0, col == TCOLS - 1)
    is_middle = jnp.logical_not(is_edge)
    outer_device = me + 2 * outer
    middle_device = me - 2 * outer
    relay_device = me + 4 * outer
    across = me + 4 * (1 - 2 * lax.div(col, 2))
    other_core = me + 1 - 2 * group
    own_slot = slot_of(0, 0)

    def load(h):
        columns = pl.ds(h * HD, HD)
        return (
            pltpu.make_async_copy(k_hbm.at[0, :, columns], kv.at[own_slot, h, 0], load_sem.at[0, h]),
            pltpu.make_async_copy(v_hbm.at[0, :, columns], kv.at[own_slot, h, 1], load_sem.at[1, h]),
            pltpu.make_async_copy(q_hbm.at[0, :, columns], q_s.at[h], load_sem.at[2, h]),
        )

    for h in range(heads):
        for copy in load(h):
            copy.start()
    w_copy = pltpu.make_async_copy(w_hbm, w_s, w_sem)
    w_copy.start()

    barrier = pltpu.get_barrier_semaphore()

    def greet(device):
        pl.semaphore_signal(barrier, inc=1, device_id={"tm": device}, device_id_type=MESH)

    greetings = jnp.int32(3)
    greet(other_core)
    greet(across)
    greet(outer_device)
    for step in (-1, 1):
        pl.when(has_time[step])(lambda step=step: greet(me + 2 * TCOLS * step))
        greetings = greetings + has_time[step].astype(jnp.int32)
    pl.when(is_middle)(lambda: greet(middle_device))
    greetings = greetings + is_middle.astype(jnp.int32)
    pl.semaphore_wait(barrier, greetings)

    def transfer(kind, h, source, target, device):
        return pltpu.make_async_remote_copy(
            src_ref=kv.at[source, h],
            dst_ref=kv.at[target, h],
            send_sem=send_sem.at[kind, h],
            recv_sem=recv_sem.at[target, h],
            device_id={"tm": device},
            device_id_type=MESH,
        )

    def arrive(slot, h):
        transfer(0, h, slot, slot, other_core).wait_recv()

    def send_time(step, h):
        return transfer(0 if step < 0 else 1, h, own_slot, slot_of(-step, 0), me + 2 * TCOLS * step)

    def send_outer(step, h):
        return transfer(3 + step, h, slot_of(step, 0), slot_of(step, 0) - outer, outer_device)

    def send_middle(step, h):
        return transfer(6 + step, h, slot_of(step, 0), slot_of(step, 0) + outer, middle_device)

    def send_relay(step, h):
        return transfer(9 + step, h, slot_of(step, 0) + outer, slot_of(step, 0) - outer, relay_device)

    def straight(step, h):
        return h >= heads - (DIRECT_OWN if step == 0 else DIRECT_CORNER)

    def send_att(h):
        return pltpu.make_async_remote_copy(
            src_ref=outgoing.at[h],
            dst_ref=attended.at[group, h],
            send_sem=att_send_sem.at[h],
            recv_sem=att_recv_sem.at[h],
            device_id={"tm": other_core},
            device_id_type=MESH,
        )

    def recv_att(h):
        return pltpu.make_async_remote_copy(
            src_ref=outgoing.at[h],
            dst_ref=attended.at[1 - group, h],
            send_sem=att_send_sem.at[h],
            recv_sem=att_recv_sem.at[h],
            device_id={"tm": other_core},
            device_id_type=MESH,
        )

    for h in range(heads):
        copies = load(h)
        copies[0].wait()
        copies[1].wait()
        for step in (-1, 1):
            pl.when(has_time[step])(lambda step=step, h=h: send_time(step, h).start())
        send_outer(0, h).start()
        if h >= heads - DIRECT_OWN:
            pl.when(is_middle)(lambda h=h: send_middle(0, h).start())

    for h in range(heads):
        load(h)[2].wait()

    exponent_scale = (HD ** (-0.5)) * LOG2E

    def attend(slot, h, first=False):
        scores = lax.dot_general(
            q_s[h], kv[slot, h, 0], (((1,), (1,)), ((), ())), preferred_element_type=jnp.float32
        )
        row_max = jnp.max(scores, axis=1, keepdims=True)
        if not first:
            old_max = m_s[h][:, :1]
            row_max = jnp.maximum(row_max, old_max)
        weights = jnp.exp2((scores - row_max) * exponent_scale)
        total = jnp.sum(weights, axis=1, keepdims=True)
        result = jnp.dot(weights.astype(jnp.bfloat16), kv[slot, h, 1], preferred_element_type=jnp.float32)
        if not first:
            keep = jnp.exp2((old_max - row_max) * exponent_scale)
            total = total + keep * l_s[h][:, :1]
            result = result + keep * acc_s[h]
        m_s[h] = jnp.broadcast_to(row_max, (rows, HD))
        l_s[h] = jnp.broadcast_to(total, (rows, HD))
        acc_s[h] = result

    def finish(h):
        acc_s[h] = acc_s[h] / l_s[h]
        attended[group, h] = acc_s[h, pl.ds(pl.multiple_of(group * half, 16), half), :].astype(jnp.bfloat16)
        outgoing[h] = acc_s[h, pl.ds(pl.multiple_of((1 - group) * half, 16), half), :].astype(jnp.bfloat16)

    @pl.loop(0, heads + LAG)
    def _(i):
        @pl.when(i < heads)
        def _():
            for step in (-1, 1):

                @pl.when(has_time[step])
                def _():
                    arrive(slot_of(step, 0), i)
                    send_outer(step, i).start()
                    if DIRECT_CORNER:
                        pl.when(jnp.logical_and(is_middle, straight(step, i)))(
                            lambda: send_middle(step, i).start()
                        )

            @pl.when(is_edge)
            def _():
                arrive(own_slot + outer, i)
                pl.when(jnp.logical_not(straight(0, i)))(lambda: send_relay(0, i).start())

        back = i - 1

        @pl.when(jnp.logical_and(jnp.logical_and(back >= 0, back < heads), is_edge))
        def _():
            for step in (-1, 1):

                @pl.when(has_time[step])
                def _():
                    arrive(slot_of(step, 0) + outer, back)
                    pl.when(jnp.logical_not(straight(step, back)))(lambda: send_relay(step, back).start())

        @pl.when(i < heads)
        def _():
            attend(own_slot, i, first=True)
            for step in (-1, 1):
                pl.when(has_time[step])(lambda: attend(slot_of(step, 0), i))

        @pl.when(jnp.logical_and(back >= 0, back < heads))
        def _():
            pl.when(is_middle)(lambda: arrive(own_slot + outer, back))
            attend(own_slot + outer, back)
            for step in (-1, 1):

                @pl.when(has_time[step])
                def _():
                    pl.when(is_middle)(lambda: arrive(slot_of(step, 0) + outer, back))
                    attend(slot_of(step, 0) + outer, back)

        last = i - LAG

        @pl.when(last >= 1)
        def _():
            send_att(last - 1).start()

        @pl.when(last >= 0)
        def _():
            @pl.when(is_middle)
            def _():
                arrive(own_slot - outer, last)
                attend(own_slot - outer, last)
                for step in (-1, 1):

                    @pl.when(has_time[step])
                    def _():
                        arrive(slot_of(step, 0) - outer, last)
                        attend(slot_of(step, 0) - outer, last)

            finish(last)

    send_att(heads - 1).start()
    w_copy.wait()

    for h in range(heads):
        recv_att(h).wait_recv()

    width = out_ref.shape[1]
    chunk = 512
    lhs = jnp.concatenate([attended[part, h] for part in range(2) for h in range(heads)], axis=1)

    @pl.loop(0, width // chunk)
    def _(n):
        columns = pl.ds(pl.multiple_of(n * chunk, chunk), chunk)
        out_ref[:, columns] = jnp.dot(lhs, w_s[:, columns], preferred_element_type=jnp.float32).astype(
            out_ref.dtype
        )

    @pl.loop(0, heads)
    def _(h):
        send_att(h).wait_send()
        send_outer(0, h).wait_send()
        if DIRECT_OWN:
            pl.when(jnp.logical_and(is_middle, straight(0, h)))(lambda: send_middle(0, h).wait_send())
        pl.when(jnp.logical_and(is_edge, jnp.logical_not(straight(0, h))))(
            lambda: send_relay(0, h).wait_send()
        )
        for step in (-1, 1):

            @pl.when(has_time[step])
            def _():
                send_time(step, h).wait_send()
                send_outer(step, h).wait_send()
                if DIRECT_CORNER:
                    pl.when(jnp.logical_and(is_middle, straight(step, h)))(
                        lambda: send_middle(step, h).wait_send()
                    )
                pl.when(jnp.logical_and(is_edge, jnp.logical_not(straight(step, h))))(
                    lambda: send_relay(step, h).wait_send()
                )


def per_device(query_states, key_states, value_states, out_weight):
    rows, half_width = query_states.shape[1:]
    heads = half_width // HD
    depth, width = out_weight.shape
    time_count = lax.axis_size("tm") // (2 * TCOLS)
    return pl.pallas_call(
        functools.partial(kernel, time_count, heads),
        out_shape=jax.ShapeDtypeStruct((rows // 2, width), jnp.bfloat16),
        in_specs=[pl.BlockSpec(memory_space=pl.ANY)] * 4,
        out_specs=pl.BlockSpec(memory_space=pltpu.VMEM),
        scratch_shapes=[
            pltpu.VMEM((heads, rows, HD), jnp.bfloat16),
            pltpu.VMEM((9, heads, 2, rows, HD), jnp.bfloat16),
            pltpu.VMEM((depth, width), jnp.bfloat16),
            pltpu.VMEM((heads, rows, HD), jnp.float32),
            pltpu.VMEM((heads, rows, HD), jnp.float32),
            pltpu.VMEM((heads, rows, HD), jnp.float32),
            pltpu.VMEM((heads, rows // 2, HD), jnp.bfloat16),
            pltpu.VMEM((2, heads, rows // 2, HD), jnp.bfloat16),
            pltpu.SemaphoreType.DMA((3, heads)),
            pltpu.SemaphoreType.DMA,
            pltpu.SemaphoreType.DMA((11, heads)),
            pltpu.SemaphoreType.DMA((9, heads)),
            pltpu.SemaphoreType.DMA((heads,)),
            pltpu.SemaphoreType.DMA((heads,)),
        ],
        compiler_params=pltpu.CompilerParams(
            collective_id=0, has_side_effects=True, vmem_limit_bytes=56 * 1024 * 1024
        ),
    )(query_states, key_states, value_states, out_weight)


def solution(mesh):
    in_specs = (
        P(("parts", "tm"), None, None),
        P(("parts", "tm"), None, None),
        P(("parts", "tm"), None, None),
        P(),
    )
    out_specs = P(("parts", "tm"), None)
    return jax.shard_map(
        per_device, mesh=mesh, in_specs=in_specs, out_specs=out_specs, check_vma=False
    )
```

time: 299 us -> 108 us (0.36)
  the two profiles are of different devices: /device:TPU:0 before, /device:TPU:5 now
where the time goes in v1:
time: 108 us
  Pallas kernels  105 us (97%)
  local copies, waits for them, and re-layouts  2.36 us (2%)
    pallas_call x1, Pallas kernels, per_device(): pl.pallas_call(functools.partial(kernel, time_count, heads), out_shape=ja...  105 us
    unnamed x1, local copies, waits for them, and re-layouts  2.36 us

profile of v1, /device:TPU:5, one launch (start us, length us, event | category | flops | bytes accessed | tf_op | source)
XLA Modules:
  0.0 107.5 jit_solution(14819058059580290611)
XLA Ops:
  0.0 105.1 %shard_map.46 = bf16[192,3072]{1,0:T(8,128)(2,1)} custom-call(bf16[1,384,768]{2,1,0:T(8,128)(2,1)} %q_hbm.1, bf16[1,384,768]{2,1,0:T(8,128)(2,1)} %k_hbm.1, bf16[1,384,768]{2,1,0:T(8,128)(2,1)} %v_hbm.1, bf16[1536,3072]{1,0:T(8,128)(2,1)} %w_hbm.1), custom_call_target="tpu_custom_call" | custom-call | tf_op jit(solution)/shard_map/pallas_call | solution.py:298
  105.2 2.4 %copy.6 = bf16[192,3072]{1,0:T(8,128)(2,1)} copy(bf16[192,3072]{1,0:T(8,128)(2,1)} %shard_map.46) | data formatting | bytes 2359296

commit v2 on v1

--- a/solution.py
+++ b/solution.py
@@ -12,8 +12,8 @@
 MESH = pl.DeviceIdType.MESH
 LOG2E = 1.4426950408889634
 
-DIRECT_OWN = 0
-DIRECT_CORNER = 0
+DIRECT_OWN = 2
+DIRECT_CORNER = 1
 LAG = 3
 
 

time: 108 us -> 97.3 us (0.901)
  Pallas kernels: 105 us -> 94.8 us
    pallas_call x1, Pallas kernels: 105 us -> 94.8 us  [per_device(): pl.pallas_call(functools.partial(kernel, time_count, heads), out_shape=ja...]
where the time goes in v2:
time: 97.3 us; the launch traced here: 97.1 us
  Pallas kernels  94.8 us (97%)
  local copies, waits for them, and re-layouts  2.36 us (2%)
    pallas_call x1, Pallas kernels, per_device(): pl.pallas_call(functools.partial(kernel, time_count, heads), out_shape=ja...  94.8 us
    unnamed x1, local copies, waits for them, and re-layouts  2.36 us

profile of v2, /device:TPU:5, one launch (start us, length us, event | category | flops | bytes accessed | tf_op | source)
XLA Modules:
  0.0 97.1 jit_solution(8423697776350177816)
XLA Ops:
  0.0 94.8 %shard_map.46 = bf16[192,3072]{1,0:T(8,128)(2,1)} custom-call(bf16[1,384,768]{2,1,0:T(8,128)(2,1)} %q_hbm.1, bf16[1,384,768]{2,1,0:T(8,128)(2,1)} %k_hbm.1, bf16[1,384,768]{2,1,0:T(8,128)(2,1)} %v_hbm.1, bf16[1536,3072]{1,0:T(8,128)(2,1)} %w_hbm.1), custom_call_target="tpu_custom_call" | custom-call | tf_op jit(solution)/shard_map/pallas_call | solution.py:298
  94.8 2.4 %copy.6 = bf16[192,3072]{1,0:T(8,128)(2,1)} copy(bf16[192,3072]{1,0:T(8,128)(2,1)} %shard_map.46) | data formatting | bytes 2359296

commit v3 on v2

--- a/solution.py
+++ b/solution.py
@@ -14,7 +14,10 @@
 
 DIRECT_OWN = 2
 DIRECT_CORNER = 1
-LAG = 3
+AHEAD = 2
+LAG_TIME = 2
+LAG_CORNER = 3
+LAG_MIDDLE = 5
 
 
 def slot_of(time_step, col_step):
@@ -59,12 +62,17 @@
     outer_device = me + 2 * outer
     middle_device = me - 2 * outer
     relay_device = me + 4 * outer
-    across = me + 4 * (1 - 2 * lax.div(col, 2))
     other_core = me + 1 - 2 * group
     own_slot = slot_of(0, 0)
+    stride = TCOLS
+    has_hop = {-1: tile >= stride // 2, 1: tile + stride // 2 < time_count * TCOLS}
+    is_hop = jnp.logical_and(has_hop[-1], has_hop[1])
+
+    def hop_slot(step):
+        return 9 if step < 0 else 10
 
     def load(h):
-        columns = pl.ds(h * HD, HD)
+        columns = pl.ds(pl.multiple_of(h * HD, HD), HD)
         return (
             pltpu.make_async_copy(k_hbm.at[0, :, columns], kv.at[own_slot, h, 0], load_sem.at[0, h]),
             pltpu.make_async_copy(v_hbm.at[0, :, columns], kv.at[own_slot, h, 1], load_sem.at[1, h]),
@@ -72,7 +80,7 @@
         )
 
     for h in range(heads):
-        for copy in load(h):
+        for copy in load(jnp.int32(h)):
             copy.start()
     w_copy = pltpu.make_async_copy(w_hbm, w_s, w_sem)
     w_copy.start()
@@ -82,13 +90,12 @@
     def greet(device):
         pl.semaphore_signal(barrier, inc=1, device_id={"tm": device}, device_id_type=MESH)
 
-    greetings = jnp.int32(3)
+    greetings = jnp.int32(2)
     greet(other_core)
-    greet(across)
     greet(outer_device)
     for step in (-1, 1):
-        pl.when(has_time[step])(lambda step=step: greet(me + 2 * TCOLS * step))
-        greetings = greetings + has_time[step].astype(jnp.int32)
+        pl.when(has_hop[step])(lambda step=step: greet(me + stride * step))
+        greetings = greetings + has_hop[step].astype(jnp.int32)
     pl.when(is_middle)(lambda: greet(middle_device))
     greetings = greetings + is_middle.astype(jnp.int32)
     pl.semaphore_wait(barrier, greetings)
@@ -107,7 +114,10 @@
         transfer(0, h, slot, slot, other_core).wait_recv()
 
     def send_time(step, h):
-        return transfer(0 if step < 0 else 1, h, own_slot, slot_of(-step, 0), me + 2 * TCOLS * step)
+        return transfer(0 if step < 0 else 1, h, own_slot, hop_slot(step), me + stride * step)
+
+    def send_hop(step, h):
+        return transfer(11 if step < 0 else 12, h, hop_slot(step), slot_of(-step, 0), me + stride * step)
 
     def send_outer(step, h):
         return transfer(3 + step, h, slot_of(step, 0), slot_of(step, 0) - outer, outer_device)
@@ -141,18 +151,17 @@
             device_id_type=MESH,
         )
 
-    for h in range(heads):
-        copies = load(h)
-        copies[0].wait()
-        copies[1].wait()
+    def send_own(h):
+        for copy in load(h):
+            copy.wait()
         for step in (-1, 1):
-            pl.when(has_time[step])(lambda step=step, h=h: send_time(step, h).start())
+            pl.when(has_time[step])(lambda step=step: send_time(step, h).start())
         send_outer(0, h).start()
-        if h >= heads - DIRECT_OWN:
-            pl.when(is_middle)(lambda h=h: send_middle(0, h).start())
-
-    for h in range(heads):
-        load(h)[2].wait()
+        if DIRECT_OWN:
+            pl.when(jnp.logical_and(is_middle, straight(0, h)))(lambda: send_middle(0, h).start())
+
+    for h in range(AHEAD):
+        send_own(jnp.int32(h))
 
     exponent_scale = (HD ** (-0.5)) * LOG2E
 
@@ -180,29 +189,42 @@
         attended[group, h] = acc_s[h, pl.ds(pl.multiple_of(group * half, 16), half), :].astype(jnp.bfloat16)
         outgoing[h] = acc_s[h, pl.ds(pl.multiple_of((1 - group) * half, 16), half), :].astype(jnp.bfloat16)
 
-    @pl.loop(0, heads + LAG)
+    def ready(h):
+        return jnp.logical_and(h >= 0, h < heads)
+
+    @pl.loop(0, heads + LAG_MIDDLE)
     def _(i):
-        @pl.when(i < heads)
+        pl.when(i + AHEAD < heads)(lambda: send_own(i + AHEAD))
+
+        @pl.when(jnp.logical_and(i < heads, is_edge))
+        def _():
+            arrive(own_slot + outer, i)
+            pl.when(jnp.logical_not(straight(0, i)))(lambda: send_relay(0, i).start())
+
+        @pl.when(jnp.logical_and(i < heads, is_hop))
+        def _():
+            for step in (-1, 1):
+                arrive(hop_slot(step), i)
+                send_hop(step, i).start()
+
+        crossed = i - LAG_TIME
+
+        @pl.when(ready(crossed))
         def _():
             for step in (-1, 1):
 
                 @pl.when(has_time[step])
                 def _():
-                    arrive(slot_of(step, 0), i)
-                    send_outer(step, i).start()
+                    arrive(slot_of(step, 0), crossed)
+                    send_outer(step, crossed).start()
                     if DIRECT_CORNER:
-                        pl.when(jnp.logical_and(is_middle, straight(step, i)))(
-                            lambda: send_middle(step, i).start()
+                        pl.when(jnp.logical_and(is_middle, straight(step, crossed)))(
+                            lambda: send_middle(step, crossed).start()
                         )
 
-            @pl.when(is_edge)
-            def _():
-                arrive(own_slot + outer, i)
-                pl.when(jnp.logical_not(straight(0, i)))(lambda: send_relay(0, i).start())
-
-        back = i - 1
-
-        @pl.when(jnp.logical_and(jnp.logical_and(back >= 0, back < heads), is_edge))
+        back = i - LAG_CORNER
+
+        @pl.when(jnp.logical_and(ready(back), is_edge))
         def _():
             for step in (-1, 1):
 
@@ -211,13 +233,14 @@
                     arrive(slot_of(step, 0) + outer, back)
                     pl.when(jnp.logical_not(straight(step, back)))(lambda: send_relay(step, back).start())
 
-        @pl.when(i < heads)
-        def _():
-            attend(own_slot, i, first=True)
-            for step in (-1, 1):
-                pl.when(has_time[step])(lambda: attend(slot_of(step, 0), i))
-
-        @pl.when(jnp.logical_and(back >= 0, back < heads))
+        pl.when(i < heads)(lambda: attend(own_slot, i, first=True))
+
+        @pl.when(ready(crossed))
+        def _():
+            for step in (-1, 1):
+                pl.when(has_time[step])(lambda: attend(slot_of(step, 0), crossed))
+
+        @pl.when(ready(back))
         def _():
             pl.when(is_middle)(lambda: arrive(own_slot + outer, back))
             attend(own_slot + outer, back)
@@ -228,7 +251,7 @@
                     pl.when(is_middle)(lambda: arrive(slot_of(step, 0) + outer, back))
                     attend(slot_of(step, 0) + outer, back)
 
-        last = i - LAG
+        last = i - LAG_MIDDLE
 
         @pl.when(last >= 1)
         def _():
@@ -270,6 +293,12 @@
     def _(h):
         send_att(h).wait_send()
         send_outer(0, h).wait_send()
+
+        @pl.when(is_hop)
+        def _():
+            for step in (-1, 1):
+                send_hop(step, h).wait_send()
+
         if DIRECT_OWN:
             pl.when(jnp.logical_and(is_middle, straight(0, h)))(lambda: send_middle(0, h).wait_send())
         pl.when(jnp.logical_and(is_edge, jnp.logical_not(straight(0, h))))(
@@ -302,7 +331,7 @@
         out_specs=pl.BlockSpec(memory_space=pltpu.VMEM),
         scratch_shapes=[
             pltpu.VMEM((heads, rows, HD), jnp.bfloat16),
-            pltpu.VMEM((9, heads, 2, rows, HD), jnp.bfloat16),
+            pltpu.VMEM((11, heads, 2, rows, HD), jnp.bfloat16),
             pltpu.VMEM((depth, width), jnp.bfloat16),
             pltpu.VMEM((heads, rows, HD), jnp.float32),
             pltpu.VMEM((heads, rows, HD), jnp.float32),
@@ -311,8 +340,8 @@
             pltpu.VMEM((2, heads, rows // 2, HD), jnp.bfloat16),
             pltpu.SemaphoreType.DMA((3, heads)),
             pltpu.SemaphoreType.DMA,
+            pltpu.SemaphoreType.DMA((13, heads)),
             pltpu.SemaphoreType.DMA((11, heads)),
-            pltpu.SemaphoreType.DMA((9, heads)),
             pltpu.SemaphoreType.DMA((heads,)),
             pltpu.SemaphoreType.DMA((heads,)),
         ],

time: 97.3 us -> 85.3 us (0.88)
  Pallas kernels: 94.8 us -> 82.8 us
    pallas_call x1, Pallas kernels: 94.8 us -> 82.8 us  [per_device(): pl.pallas_call(functools.partial(kernel, time_count, heads), out_shape=ja...]
where the time goes in v3:
time: 85.3 us; the launch traced here: 85.2 us
  Pallas kernels  82.8 us (97%)
  local copies, waits for them, and re-layouts  2.36 us (3%)
    pallas_call x1, Pallas kernels, per_device(): pl.pallas_call(functools.partial(kernel, time_count, heads), out_shape=ja...  82.8 us
    unnamed x1, local copies, waits for them, and re-layouts  2.36 us

profile of v3, /device:TPU:5, one launch (start us, length us, event | category | flops | bytes accessed | tf_op | source)
XLA Modules:
  0.0 85.2 jit_solution(10091741264825688948)
XLA Ops:
  0.0 82.8 %shard_map.46 = bf16[192,3072]{1,0:T(8,128)(2,1)} custom-call(bf16[1,384,768]{2,1,0:T(8,128)(2,1)} %q_hbm.1, bf16[1,384,768]{2,1,0:T(8,128)(2,1)} %k_hbm.1, bf16[1,384,768]{2,1,0:T(8,128)(2,1)} %v_hbm.1, bf16[1536,3072]{1,0:T(8,128)(2,1)} %w_hbm.1), custom_call_target="tpu_custom_call" | custom-call | tf_op jit(solution)/shard_map/pallas_call | solution.py:327
  82.8 2.4 %copy.6 = bf16[192,3072]{1,0:T(8,128)(2,1)} copy(bf16[192,3072]{1,0:T(8,128)(2,1)} %shard_map.46) | data formatting | bytes 2359296

commit v4 on v3

--- a/solution.py
+++ b/solution.py
@@ -282,7 +282,7 @@
     chunk = 512
     lhs = jnp.concatenate([attended[part, h] for part in range(2) for h in range(heads)], axis=1)
 
-    @pl.loop(0, width // chunk)
+    @pl.loop(0, width // chunk, unroll=True)
     def _(n):
         columns = pl.ds(pl.multiple_of(n * chunk, chunk), chunk)
         out_ref[:, columns] = jnp.dot(lhs, w_s[:, columns], preferred_element_type=jnp.float32).astype(

time: 85.3 us -> 84.4 us (0.989)
  Pallas kernels: 82.8 us -> 81.9 us
    pallas_call x1, Pallas kernels: 82.8 us -> 81.9 us  [per_device(): pl.pallas_call(functools.partial(kernel, time_count, heads), out_shape=ja...]
where the time goes in v4:
time: 84.4 us; the launch traced here: 84.3 us
  Pallas kernels  81.9 us (97%)
  local copies, waits for them, and re-layouts  2.36 us (3%)
    pallas_call x1, Pallas kernels, per_device(): pl.pallas_call(functools.partial(kernel, time_count, heads), out_shape=ja...  81.9 us
    unnamed x1, local copies, waits for them, and re-layouts  2.36 us

profile of v4, /device:TPU:5, one launch (start us, length us, event | category | flops | bytes accessed | tf_op | source)
XLA Modules:
  0.0 84.3 jit_solution(7690222524487722975)
XLA Ops:
  0.0 81.9 %shard_map.46 = bf16[192,3072]{1,0:T(8,128)(2,1)} custom-call(bf16[1,384,768]{2,1,0:T(8,128)(2,1)} %q_hbm.1, bf16[1,384,768]{2,1,0:T(8,128)(2,1)} %k_hbm.1, bf16[1,384,768]{2,1,0:T(8,128)(2,1)} %v_hbm.1, bf16[1536,3072]{1,0:T(8,128)(2,1)} %w_hbm.1), custom_call_target="tpu_custom_call" | custom-call | tf_op jit(solution)/shard_map/pallas_call | solution.py:327
  81.9 2.4 %copy.6 = bf16[192,3072]{1,0:T(8,128)(2,1)} copy(bf16[192,3072]{1,0:T(8,128)(2,1)} %shard_map.46) | data formatting | bytes 2359296
